TPU v7x, 256 devices: a whole 4x4x8 slice. The times are simulated.
256 devices in a mesh: grp: 8 (over y, core), dev: 32 (over z, x).
Axes of the slice: x: 4, y: 4, z: 8, core: 2. Of those that a mesh axis runs over, the one named last changes fastest.
Arguments:
- charges: bfloat16 [8192, 16, 128], P(('grp', 'dev')), may hold values from -6 to 6
- leaf_basis: bfloat16 [8192, 128, 64], P(('grp', 'dev')), may hold values from -0.5 to 0.5
- near_blocks: bfloat16 [40960, 128, 128], P(('grp', 'dev')), may hold values from -0.375 to 0.375
- near_target: int32 [40960], P(('grp', 'dev')), may hold values from 0 to 8191, as said below
- near_source: int32 [40960], P(('grp', 'dev')), may hold values from 0 to 8191, as said below
- near_count: int32 [256], P(('grp', 'dev')), may hold values from 40 to 160, as said below
- leaf_far: int32 [8192, 16], P(('grp', 'dev')), may hold values from 0 to 8191, as said below
- leaf_far_couple: int32 [8192, 16], P(('grp', 'dev')), may hold values from 0 to 315
- leaf_trans: int32 [8192], P(('grp', 'dev')), may hold values from 0 to 7
- dev_trans: int32 [256], P(('grp', 'dev')), may hold values from 0 to 7
- dev_list: int32 [256, 4], P(('grp', 'dev')), may hold values from 0 to 255, as said below
- dev_couple: int32 [256, 4], P(('grp', 'dev')), may hold values from 0 to 315
- grp_couple: int32 [8, 8], replicated, may hold values from 0 to 315
- trans_leaf: float32 [8, 64, 64], replicated, may hold values from -0.375 to 0.375
- trans_dev: float32 [8, 64, 64], replicated, may hold values from -0.25 to 0.25
- couple_table: float32 [316, 64, 64], replicated, may hold values from -0.375 to 0.375
Outputs:
- potentials: float32 [8192, 16, 128], P(('grp', 'dev'))
Inputs may be any that keep to these rules, and one draw needn't show every extreme that they name: `near_count`: live slots of a device are at least a quarter of its 160; some device has all slots live and some device exactly 40. `near_target`: slot s names a leaf of device s // 160. `near_source`: slot s names a leaf within 16 leaves of device s // 160's range of leaves; on every device both ends of that window are named where they exist. `leaf_far`: leaf b names leaves within 16 leaves of the range of its device; on every device both ends of that window are named where they exist. `dev_list`: box d names boxes of its own subtree, never itself nor the two next to it in cyclic order within the subtree.
All inputs are finite; a program needn't handle non-finite values.
Results may differ from a plain program's by a relative error of at most 0.0024.
Values may be sent and summed in bfloat16 or wider, within the bound.
A program may use at most 128 MiB of HBM per device.

v0:
```python
import jax
import jax.numpy as jnp
from jax import lax
from jax.sharding import PartitionSpec as P

HIGHEST = lax.Precision.HIGHEST


def padded(block, sides, width):
    for axis, dim in sides:
        count = lax.axis_size(axis)
        forward = [(i, i + 1) for i in range(count - 1)]
        backward = [(target, source) for source, target in forward]
        low = lax.ppermute(
            lax.slice_in_dim(block, block.shape[dim] - width, None, axis=dim), axis, forward
        )
        high = lax.ppermute(lax.slice_in_dim(block, 0, width, axis=dim), axis, backward)
        block = jnp.concatenate([low, block, high], axis=dim)
    return block


def near_slots(source_rows, blocks, targets, picks, live, leaf_start, leaves):
    picked = source_rows[picks]
    product = jnp.einsum("sij,srj->sri", blocks, picked, preferred_element_type=jnp.float32)
    local_target = targets - leaf_start
    onehot = ((local_target[None, :] == jnp.arange(leaves)[:, None]) & live[None, :]).astype(
        jnp.float32
    )
    return jnp.einsum("ts,sri->tri", onehot, product, precision=HIGHEST)


def local(
    charges,
    leaf_basis,
    near_blocks,
    near_target,
    near_source,
    near_count,
    leaf_far,
    leaf_far_couple,
    leaf_trans,
    dev_trans,
    dev_list,
    dev_couple,
    grp_couple,
    trans_leaf,
    trans_dev,
    couple_table,
):
    leaves = charges.shape[0]
    margin = leaves // 2
    slot_total = near_blocks.shape[0]
    per_group = lax.axis_size("dev")
    group_index = lax.axis_index("grp")
    box_index = group_index * per_group + lax.axis_index("dev")
    leaf_start = box_index * leaves
    window = padded(charges, ((("grp", "dev"), 0),), margin)
    leaf_moment = jnp.einsum(
        "lrp,lpk->lrk", charges, leaf_basis, preferred_element_type=jnp.float32
    )
    moment_window = padded(leaf_moment, ((("grp", "dev"), 0),), margin)
    child_maps = trans_leaf[leaf_trans]
    box_moment = jnp.einsum("lrk,lkj->rj", leaf_moment, child_maps, precision=HIGHEST)
    moments, kinds = (
        lax.all_gather(box_moment[None], ("grp", "dev"), axis=0, tiled=True),
        lax.all_gather(dev_trans, ("grp", "dev"), axis=0, tiled=True),
    )
    groups = moments.shape[0] // per_group
    up_all = trans_dev[kinds]
    group_moment = jnp.einsum(
        "gdrk,gdkj->grj",
        moments.reshape(groups, per_group, moments.shape[1], moments.shape[2]),
        up_all.reshape(groups, per_group, up_all.shape[1], up_all.shape[2]),
        precision=HIGHEST,
    )
    peers = lax.dynamic_slice_in_dim(moments, group_index * per_group, per_group, 0)
    groups = group_moment.shape[0]
    away = (jnp.arange(groups) != group_index).astype(jnp.float32)
    group_local = jnp.einsum(
        "h,hrk,hkj->rj",
        away,
        group_moment,
        couple_table[grp_couple[group_index]],
        precision=HIGHEST,
    )
    own_up = trans_dev[dev_trans[0]]
    box_local = jnp.einsum("rj,kj->rk", group_local, own_up, precision=HIGHEST)
    listed = peers[dev_list[0] - group_index * per_group]
    box_local = box_local + jnp.einsum(
        "nrk,nkj->rj", listed, couple_table[dev_couple[0]], precision=HIGHEST
    )
    far_moments = moment_window[leaf_far - leaf_start + margin]
    far_terms = jnp.einsum(
        "lfrk,lfkj->lrj", far_moments, couple_table[leaf_far_couple], precision=HIGHEST
    )
    leaf_local = jnp.einsum("rj,lkj->lrk", box_local, child_maps, precision=HIGHEST) + far_terms
    leaf_local = leaf_local.astype(jnp.bfloat16)
    far_part = jnp.einsum(
        "lrk,lpk->lrp", leaf_local, leaf_basis, preferred_element_type=jnp.float32
    )
    live = jnp.arange(slot_total) < near_count[0]
    near_part = near_slots(
        window,
        near_blocks,
        near_target,
        near_source - leaf_start + margin,
        live,
        leaf_start,
        leaves,
    )
    return near_part + far_part


def solution(mesh):
    return jax.shard_map(
        local,
        mesh=mesh,
        in_specs=(
            P(("grp", "dev"), None, None),
            P(("grp", "dev"), None, None),
            P(("grp", "dev"), None, None),
            P(("grp", "dev")),
            P(("grp", "dev")),
            P(("grp", "dev")),
            P(("grp", "dev"), None),
            P(("grp", "dev"), None),
            P(("grp", "dev")),
            P(("grp", "dev")),
            P(("grp", "dev"), None),
            P(("grp", "dev"), None),
            P(),
            P(),
            P(),
            P(),
        ),
        out_specs=P(("grp", "dev"), None, None),
        check_vma=False,
    )
```

profile of v0, /device:TPU:1, one launch (start us, length us, event | category | flops | bytes accessed | tf_op | source)
XLA Modules:
  0.0 209.0 jit_solution(11731848971093460624)
XLA Ops:
  7.6 1.3 fusion.26
  8.9 1.6 gather_fusion.1
  10.5 1.3 convolution_bitcast_fusion.5
  11.8 3.9 %collective-permute-start.2 = (f32[16,16,64]{2,1,0:T(8,128)S(1)}, f32[16,16,64]{2,1,0:T(8,128)S(1)}, u32[]{:S(2)}, u32[]{:S(2)}) collective-permute-start(f32[16,16,64]{2,1,0:T(8,128)S(1)} %get-tuple-element.5), channel_id=1, source_target_pairs={{0,1},{1,2},{2,3},{3,4},{4,5},{5,6},{6,7},{7,8},{8,9},{9,10},{10,1... | collective-permute-start | bytes 196616 | tf_op jit(solution)/shard_map/ppermute | solution.py:14
  15.7 9.0 %collective-permute-start.3 = (f32[16,16,64]{2,1,0:T(8,128)S(1)}, f32[16,16,64]{2,1,0:T(8,128)}, u32[]{:S(2)}, u32[]{:S(2)}) collective-permute-start(f32[16,16,64]{2,1,0:T(8,128)S(1)} %get-tuple-element.6), channel_id=1, source_target_pairs={{1,0},{2,1},{3,2},{4,3},{5,4},{6,5},{7,6},{8,7},{9,8},{10,9},{11,1... | collective-permute-start | bytes 196616 | tf_op jit(solution)/shard_map/ppermute | solution.py:17
  24.8 1.5 fusion.24
  26.3 1.9 collective-permute-start
  28.2 7.0 %collective-permute-start.1 = (bf16[16,16,128]{2,1,0:T(8,128)(2,1)}, bf16[16,16,128]{2,1,0:T(8,128)(2,1)}, u32[]{:S(2)}, u32[]{:S(2)}) collective-permute-start(bf16[16,16,128]{2,1,0:T(8,128)(2,1)} %get-tuple-element.8), channel_id=1, source_target_pairs={{1,0},{2,1},{3,2},{4,3},{5,4},{6,5},{7,6},{8,7},{9,8},{10,9},{11,1... | collective-permute-start | bytes 196616 | tf_op jit(solution)/shard_map/ppermute | solution.py:17
  35.9 12.3 %copy.19 = f32[316,64,64]{2,1,0:T(8,128)} copy(f32[316,64,64]{0,2,1:T(8,128)} %param.31) | data formatting | bytes 10354688 | tf_op args[15]
  49.1 74.2 %all-reduce = s32[256]{0:T(256)S(1)} all-reduce(s32[256]{0:T(256)S(1)} %dynamic-update-slice), channel_id=1, replica_groups=mesh['grp'=8,'dev'=32] {'grp','dev'}, use_global_device_ids=true, to_apply=%add | all-reduce | flops 256 | bytes 2048
  123.3 4.5 %gather_fusion.3 = f32[8,64,64]{2,1,0:T(8,128)S(1)} fusion(f32[316,64,64]{2,1,0:T(8,128)} %copy.19, s32[1024]{0:T(1024)S(1)} %pad_clamp_fusion.4), kind=kCustom, calls=%fused_computation.3 | custom fusion | bytes 262176 | tf_op jit(solution)/shard_map/gather | solution.py:83
  127.8 4.5 %gather_fusion.5 = f32[4,64,64]{2,1,0:T(8,128)S(1)} fusion(f32[316,64,64]{2,1,0:T(8,128)} %copy.19, s32[1024]{0:T(1024)S(1)} %pad_clamp_fusion.2), kind=kCustom, calls=%fused_computation.5 | custom fusion | bytes 131088 | tf_op jit(solution)/shard_map/gather | solution.py:90
  132.7 25.0 %gather_fusion.7 = f32[512,64,64]{2,1,0:T(8,128)} fusion(f32[316,64,64]{2,1,0:T(8,128)} %copy.19, s32[1024]{0:T(1024)S(1)} %pad_clamp_fusion), kind=kCustom, calls=%fused_computation.7 | custom fusion | bytes 16779264 | tf_op jit(solution)/shard_map/gather | solution.py:94
  158.4 4.4 %gather_fusion.2 = f32[256,64,64]{2,1,0:T(8,128)} fusion(f32[8,64,64]{2,1,0:T(8,128)S(1)} %copy-done.1, s32[1024]{0:T(1024)S(1)} %pad_clamp_fusion.5), kind=kCustom, calls=%fused_computation.2 | custom fusion | bytes 8389632 | tf_op jit(solution)/shard_map/gather | solution.py:69
  164.0 0.9 pad_maximum_fusion
  164.9 3.1 %gather_fusion.6 = f32[512,16,64]{2,1,0:T(8,128)} fusion(f32[64,16,64]{2,1,0:T(8,128)S(1)} %pad_maximum_fusion, s32[1024]{0:T(1024)S(1)} %pad_clamp_fusion.1), kind=kCustom, calls=%fused_computation.6 | custom fusion | bytes 4196352 | tf_op jit(solution)/shard_map/gather | solution.py:92
  168.1 0.9 pad_maximum_fusion.1
  169.7 6.4 %fusion.25 = f32[160,16,128]{2,1,0:T(8,128)} fusion(bf16[160,16,128]{2,1,0:T(8,128)(2,1)S(1)} %gather_fusion, bf16[160,128,128]{2,1,0:T(8,128)(2,1)} %param.18), kind=kOutput, calls=%fused_computation.60 | convolution fusion | flops 83886080 | bytes 7208960 | tf_op jit(solution)/shard_map/sij,srj->sri/dot_general | solution.py:24
  176.1 7.1 %fusion.7 = f32[8,16,64]{2,1,0:T(8,128)S(1)} fusion(f32[8,32,16,64]{3,2,1,0:T(8,128)} %bitcast.81, f32[8,32,64,64]{3,2,1,0:T(8,128)} %bitcast.79, f32[8]{0:T(128)S(1)} %copy-done.9), kind=kOutput, calls=%fused_computation.16 | convolution fusion | flops 201334784 | bytes 5275680 | tf_op jit(solution)/shard_map/gdrk,gdkj->grj/dot_general | solution.py:70
  183.6 1.0 constant_dynamic-slice_fusion
  185.4 2.5 %convolution_bitcast_fusion.1 = f32[32,16,64]{2,1,0:T(8,128)S(1)} fusion(f32[32,64,64]{2,1,0:T(8,128)S(1)} %gather_fusion.1, f32[16,64,1]{1,0,2:T(8,128)S(1)} %fusion.9), kind=kOutput, calls=%fused_computation.12 | convolution fusion | flops 25165824 | bytes 659456 | tf_op jit(solution)/shard_map/rj,lkj->lrk/dot_general | solution.py:96
  188.0 12.1 %fusion.6 = bf16[32,16,64]{2,1,0:T(8,128)(2,1)S(1)} fusion(f32[32,16,64]{2,1,0:T(8,128)S(1)} %convolution_bitcast_fusion.1, f32[32,16,16,64]{3,2,1,0:T(8,128)} %bitcast.80, f32[32,16,64,64]{3,2,1,0:T(8,128)} %bitcast.78), kind=kOutput, calls=%fused_computation.14 | convolution fusion | flops 402718720 | bytes 10682368 | tf_op jit(solution)/shard_map/lfrk,lfkj->lrj/dot_general | solution.py:93
  200.4 0.9 fusion.3
  201.3 0.9 copy.25
  (63 shorter events, 5.7 us)
Async XLA Ops:
  6.5 1.1 copy-start
  6.5 169.6 %all-gather.3.cloned.1.call-start = ((), (), s32[]{:S(2)}) async-start(), calls=%async_computation | async-start | bytes 2105344 | tf_op jit(solution)/shard_map/all_gather | solution.py:65
  11.8 152.2 %collective-permute-start.2 = (f32[16,16,64]{2,1,0:T(8,128)S(1)}, f32[16,16,64]{2,1,0:T(8,128)S(1)}, u32[]{:S(2)}, u32[]{:S(2)}) collective-permute-start(f32[16,16,64]{2,1,0:T(8,128)S(1)} %get-tuple-element.5), channel_id=1, source_target_pairs={{0,1},{1,2},{2,3},{3,4},{4,5},{5,6},{6,7},{7,8},{8,9},{9,10},{10,1... | collective-permute-start | bytes 196616 | tf_op jit(solution)/shard_map/ppermute | solution.py:14
  15.7 148.3 %collective-permute-start.3 = (f32[16,16,64]{2,1,0:T(8,128)S(1)}, f32[16,16,64]{2,1,0:T(8,128)}, u32[]{:S(2)}, u32[]{:S(2)}) collective-permute-start(f32[16,16,64]{2,1,0:T(8,128)S(1)} %get-tuple-element.6), channel_id=1, source_target_pairs={{1,0},{2,1},{3,2},{4,3},{5,4},{6,5},{7,6},{8,7},{9,8},{10,9},{11,1... | collective-permute-start | bytes 196616 | tf_op jit(solution)/shard_map/ppermute | solution.py:17
  26.3 141.7 %collective-permute-start = (bf16[16,16,128]{2,1,0:T(8,128)(2,1)}, bf16[16,16,128]{2,1,0:T(8,128)(2,1)}, u32[]{:S(2)}, u32[]{:S(2)}) collective-permute-start(bf16[16,16,128]{2,1,0:T(8,128)(2,1)} %get-tuple-element.7), channel_id=1, source_target_pairs={{0,1},{1,2},{2,3},{3,4},{4,5},{5,6},{6,7},{7,8},{8,9},{9,10},{10,1... | collective-permute-start | bytes 196616 | tf_op jit(solution)/shard_map/ppermute | solution.py:14
  28.2 139.8 %collective-permute-start.1 = (bf16[16,16,128]{2,1,0:T(8,128)(2,1)}, bf16[16,16,128]{2,1,0:T(8,128)(2,1)}, u32[]{:S(2)}, u32[]{:S(2)}) collective-permute-start(bf16[16,16,128]{2,1,0:T(8,128)(2,1)} %get-tuple-element.8), channel_id=1, source_target_pairs={{1,0},{2,1},{3,2},{4,3},{5,4},{6,5},{7,6},{8,7},{9,8},{10,9},{11,1... | collective-permute-start | bytes 196616 | tf_op jit(solution)/shard_map/ppermute | solution.py:17
  35.9 87.4 %copy-start.10 = (s32[1,4]{1,0:T(1,128)S(1)}, s32[1,4]{1,0:T(1,128)}, u32[]{:S(2)}) copy-start(s32[1,4]{1,0:T(1,128)} %param.27) | copy-start | bytes 52
  35.9 96.4 %copy-start.4 = (s32[32,16]{0,1:T(8,128)S(1)}, s32[32,16]{0,1:T(8,128)}, u32[]{:S(2)}) copy-start(s32[32,16]{0,1:T(8,128)} %param.22) | copy-start | bytes 6148
  35.9 96.6 %copy-start.5 = (s32[32,16]{0,1:T(8,128)S(1)}, s32[32,16]{0,1:T(8,128)}, u32[]{:S(2)}) copy-start(s32[32,16]{0,1:T(8,128)} %param.23) | copy-start | bytes 6148
  132.7 25.7 %copy-start.1 = (f32[8,64,64]{2,1,0:T(8,128)S(1)}, f32[8,64,64]{2,1,0:T(8,128)}, u32[]{:S(2)}) copy-start(f32[8,64,64]{2,1,0:T(8,128)} %param.30) | copy-start | bytes 393220
  158.4 4.9 %copy-start.11 = (s32[1,4]{1,0:T(1,128)S(1)}, s32[1,4]{1,0:T(1,128)}, u32[]{:S(2)}) copy-start(s32[1,4]{1,0:T(1,128)} %param.26) | copy-start | bytes 52
  158.4 5.0 %copy-start.6 = (s32[160]{0:T(256)S(1)}, s32[160]{0:T(256)}, u32[]{:S(2)}) copy-start(s32[160]{0:T(256)} %param.20) | copy-start | bytes 1924
  158.4 5.0 %copy-start.7 = (s32[160]{0:T(256)S(1)}, s32[160]{0:T(256)}, u32[]{:S(2)}) copy-start(s32[160]{0:T(256)} %param.19) | copy-start | bytes 1924
  162.8 5.3 %copy-start.3 = (bf16[32,16,128]{2,1,0:T(8,128)(2,1)S(1)}, bf16[32,16,128]{2,1,0:T(8,128)(2,1)}, u32[]{:S(2)}) copy-start(bf16[32,16,128]{2,1,0:T(8,128)(2,1)} %param.16) | copy-start | bytes 393220
  168.0 8.1 %copy-start.9 = (f32[8]{0:T(128)S(1)}, f32[8]{0:T(128)}, u32[]{:S(2)}) copy-start(f32[8]{0:T(128)} %compare_convert_fusion) | copy-start | bytes 100
  188.0 12.4 %copy-start.2 = (f32[160,16,128]{2,1,0:T(8,128)S(1)}, f32[160,16,128]{2,1,0:T(8,128)}, u32[]{:S(2)}) copy-start(f32[160,16,128]{2,1,0:T(8,128)} %fusion.25) | copy-start | bytes 3932164
  188.0 12.4 %copy-start.8 = (pred[160]{0:T(512)(128)(4,1)S(1)}, pred[160]{0:T(512)(128)(4,1)}, u32[]{:S(2)}) copy-start(pred[160]{0:T(512)(128)(4,1)} %iota_compare_fusion.1) | copy-start | bytes 484
Sparse Core Ops, SparseCore 0:
  11.9 108.3 all-gather.2
where the time goes:
time: 210 us; the launch traced here: 209 us
  blocking collectives  74.2 us (35%)
  local copies, waits for them, and re-layouts  60.9 us (29%)
  matrix products  32.5 us (15%)
  starting transfers between devices  21.9 us (10%)
  between operations  15 us (7%)
  other arithmetic  4.47 us (2%)
    unnamed x1, blocking collectives  74.2 us
    gather x1, local copies, waits for them, and re-layouts, local(): couple_table[leaf_far_couple]  25 us
    ppermute x2, starting transfers between devices, padded(): lax.ppermute(lax.slice_in_dim(block, 0, width, axis=dim), axis, backward)  16 us
    unnamed x27, local copies, waits for them, and re-layouts  12.8 us
    dot_general x1, matrix products, local(): jnp.einsum('lfrk,lfkj->lrj', far_moments, couple_table[leaf_far_couple],...  12.1 us
    dot_general x1, matrix products, local(): jnp.einsum('gdrk,gdkj->grj', moments.reshape(groups, per_group, moments.s...  7.09 us
    dot_general x1, matrix products, near_slots(): jnp.einsum('sij,srj->sri', blocks, picked, preferred_element_type=jnp.flo...  6.4 us
    ppermute x2, starting transfers between devices, padded(): lax.ppermute(lax.slice_in_dim(block, block.shape[dim] - width, None, axis...  5.85 us
  transfers between devices with their start and end apart: 5, of which 0 were waited for; matrix products, arithmetic and copies ran while one was open for 32% of the time, Pallas kernels for 0%

commit v1 on v0

v1 whole, which is shorter than its diff:
```python
import functools

import jax
import jax.numpy as jnp
from jax import lax
from jax.experimental import pallas as pl
from jax.experimental.pallas import tpu as pltpu
from jax.sharding import PartitionSpec as P

f32, bf16 = jnp.float32, jnp.bfloat16
MESH = pl.DeviceIdType.MESH
NT = (((1,), (1,)), ((), ()))


def split(x):
    high = x.astype(bf16)
    return high, (x - high.astype(f32)).astype(bf16)


def inside(index, size):
    return lax.min(lax.max(index, 0), size - 1)


def left_half(shape):
    return lax.broadcasted_iota(jnp.int32, shape, 1) < 64


def compact(doubled):
    high, low = split(doubled)
    return jnp.where(left_half(high.shape), high.astype(f32), low.astype(f32)).astype(bf16)


def doubled_sum(total):
    return total + pltpu.roll(total, 64, 1)


def spread_matrix():
    row = lax.broadcasted_iota(jnp.int32, (128, 512), 0)
    column = lax.broadcasted_iota(jnp.int32, (128, 512), 1)
    hit = (row >> 5 == column >> 7) & (row & 31 == column & 31)
    return hit.astype(f32).astype(bf16)


def spread(blocks, matrix):
    wide = jnp.dot(blocks, matrix, preferred_element_type=f32).astype(bf16)
    out = []
    for i in range(blocks.shape[0] // 16):
        rows = wide[i * 16 : (i + 1) * 16]
        out.append(jnp.concatenate([rows[:, g * 128 : (g + 1) * 128] for g in range(4)], axis=0))
    return out


def times_maps(wide, maps):
    weights = []
    for m in maps:
        weights.extend(split(m))
    weights = jnp.concatenate(weights, axis=0)
    if len(wide) == 1:
        lanes = wide[0][:, :64]
    else:
        half = left_half((64, 128))
        lanes = jnp.concatenate(
            [jnp.where(half, wide[i], wide[i + 1]) for i in range(0, len(wide), 2)], axis=1
        )
    return jnp.dot(lanes, weights, preferred_element_type=f32)


def fold(total):
    kept = jnp.where(
        left_half((16, 128)), total[0:16] + total[32:48], total[16:32] + total[48:64]
    )
    return doubled_sum(kept)


def kernel(
    sizes,
    charges,
    basis,
    blocks,
    target,
    source,
    count,
    far,
    far_couple,
    leaf_trans,
    dev_trans,
    dev_list,
    dev_couple,
    grp_couple,
    trans_leaf,
    trans_dev,
    couple,
    out,
    window,
    bt,
    blk,
    tl,
    td,
    raw,
    table,
    small,
    small_t,
    cwin,
    mwin,
    ubuf,
    xbuf,
    zbuf,
    bbuf,
    usend,
    vsend,
    wsend,
    prod,
    nbuf,
    farb,
    ybuf,
    local_sem,
    chunk_sem,
    halo_send,
    halo_recv,
    u_send,
    u_recv,
    x_send,
    x_recv,
    bx_send,
    bx_recv,
    z_send,
    z_recv,
    bz_send,
    bz_recv,
):
    groups, zs, xs = sizes
    per_group = zs * xs
    leaves = out.shape[0]
    margin = leaves // 2
    slots = blk.shape[0]
    types = table.shape[0]
    rows_of = table.reshape(types * 32, 128)
    ntrans = tl.shape[0]
    chunks = 4
    per_chunk = 32 // chunks
    g, d = lax.axis_index("grp"), lax.axis_index("dev")
    z, x = lax.div(d, xs), lax.rem(d, xs)
    me = g * per_group + d
    total = groups * per_group
    right, left = lax.rem(me + 1, total), lax.rem(me + total - 1, total)
    first = me * leaves - margin

    def at(index):
        return {"grp": lax.div(index, per_group), "dev": lax.rem(index, per_group)}

    def group_peer(o):
        return {"grp": lax.rem(g + o, groups), "dev": d}

    def x_peer(o):
        return {"grp": g, "dev": z * xs + lax.rem(x + o, xs)}

    def z_peer(o):
        return {"grp": g, "dev": lax.rem(z + o, zs) * xs + x}

    loads = []
    for i, (a, b) in enumerate(
        (
            (charges, window.at[pl.ds(margin, leaves)]),
            (basis, bt),
            (trans_leaf, tl),
            (trans_dev, td),
        )
    ):
        loads.append(pltpu.make_async_copy(a, b, local_sem.at[i]))
    raw_loads = []
    for c in range(chunks):
        for half in range(2):
            rows = pl.ds(half * 32 + c * per_chunk, per_chunk)
            raw_loads.append(
                pltpu.make_async_copy(couple.at[rows], raw.at[rows], chunk_sem.at[c * 2 + half])
            )
    block_load = pltpu.make_async_copy(blocks, blk, local_sem.at[4])
    for copy in loads + raw_loads + [block_load]:
        copy.start()

    barrier = pltpu.get_barrier_semaphore()
    peers = (
        [at(left), at(right)]
        + [group_peer(o) for o in range(1, groups)]
        + [x_peer(o) for o in range(1, xs)]
        + [z_peer(o) for o in range(1, zs)]
    )
    for peer in peers:
        pl.semaphore_signal(barrier, inc=1, device_id=peer, device_id_type=MESH)

    matrix = spread_matrix()
    loads[2].wait()
    loads[3].wait()
    for i in range(2 * ntrans):
        m = tl[i] if i < ntrans else td[i - ntrans]
        small[i] = jnp.concatenate([m[:32], m[32:]], axis=1)
        small_t[i] = compact(jnp.concatenate([m, m], axis=1))

    loads[0].wait()
    loads[1].wait()

    def moments(step, carry):
        for j in range(8):
            leaf = step * 8 + j
            b = bt[leaf]
            m = lax.dot_general(
                window[margin + leaf],
                jnp.concatenate([b, b], axis=0),
                NT,
                preferred_element_type=f32,
            )
            cwin[margin + leaf] = compact(m)
        return carry

    lax.fori_loop(0, leaves // 8, moments, 0)

    def widen(start):
        def body(step, carry):
            c = jnp.concatenate([cwin[start + step * 8 + j] for j in range(8)], axis=0)
            for j, w in enumerate(spread(c, matrix)):
                mwin[start + step * 8 + j] = w
            return carry

        return body

    lax.fori_loop(0, leaves // 8, widen(margin), 0)

    def small_map(i):
        return small[i]

    def big_map(i):
        return table[i]

    def to_box(step, carry):
        picks = [step * 4 + j for j in range(4)]
        return carry + times_maps(
            [mwin[margin + p] for p in picks], [small_map(leaf_trans[p]) for p in picks]
        )

    box = compact(fold(lax.fori_loop(0, leaves // 4, to_box, jnp.zeros((64, 128), f32))))
    bbuf[d] = box
    dtrans = dev_trans[0]
    usend[...] = compact(fold(times_maps(spread(box, matrix), [small_map(ntrans + dtrans)])))
    ubuf[g] = jnp.zeros((16, 128), bf16)

    pl.semaphore_wait(barrier, len(peers))

    def remote(src, dst, send, recv, i, peer):
        copy = pltpu.make_async_remote_copy(
            src_ref=src,
            dst_ref=dst,
            send_sem=send.at[i],
            recv_sem=recv.at[i],
            device_id=peer,
            device_id_type=MESH,
        )
        copy.start()
        return copy

    to_groups = [
        remote(usend, ubuf.at[g], u_send, u_recv, o - 1, group_peer(o)) for o in range(1, groups)
    ]
    box_x = [
        remote(bbuf.at[d], bbuf.at[d], bx_send, bx_recv, o - 1, x_peer(o))
        for o in range(1, xs)
    ]
    low, high = pl.ds(0, margin), pl.ds(leaves, margin)
    end_low, end_high = pl.ds(margin + leaves, margin), pl.ds(margin, margin)
    charge_halo = [
        remote(charges.at[pl.ds(leaves - margin, margin)], window.at[low], halo_send, halo_recv, 0, at(right)),
        remote(charges.at[pl.ds(0, margin)], window.at[end_low], halo_send, halo_recv, 1, at(left)),
    ]
    moment_halo = [
        remote(cwin.at[high], cwin.at[low], halo_send, halo_recv, 2, at(right)),
        remote(cwin.at[end_high], cwin.at[end_low], halo_send, halo_recv, 3, at(left)),
    ]

    for c in range(chunks):
        raw_loads[2 * c].wait()
        raw_loads[2 * c + 1].wait()

        def turn(i, carry):
            k = c * per_chunk + i
            both = jnp.concatenate([raw[k], raw[k + 32]], axis=0)
            rows_of[pl.ds(k, types, stride=32), :] = both.T
            return carry

        lax.fori_loop(0, per_chunk, turn, 0)

    for copy in to_groups:
        copy.wait_recv()
    share = jnp.zeros((64, 128), f32)
    for h in range(0, groups, 4):
        picks = list(range(h, min(h + 4, groups)))
        rows = jnp.concatenate([ubuf[p] for p in picks], axis=0)
        share = share + times_maps(spread(rows, matrix), [big_map(grp_couple[g, p]) for p in picks])
    vsend[...] = compact(fold(share))
    xbuf[x] = vsend[...]
    share_x = [
        remote(vsend, xbuf.at[x], x_send, x_recv, o - 1, x_peer(o)) for o in range(1, xs)
    ]
    for copy in box_x:
        copy.wait_recv()
    plane = pl.ds(z * xs, xs)
    box_z = [
        remote(bbuf.at[plane], bbuf.at[plane], bz_send, bz_recv, o - 1, z_peer(o)) for o in range(1, zs)
    ]

    for copy in charge_halo:
        copy.wait_recv()
    block_load.wait()

    def near(step, carry):
        for j in range(8):
            s = step * 8 + j
            product = lax.dot_general(
                window[inside(source[s] - first, 2 * leaves)], blk[s], NT, preferred_element_type=f32
            )
            prod[pl.ds(pl.multiple_of(s * 16, 16), 16), :] = product
        return carry

    half_slots = slots // 16
    lax.fori_loop(0, half_slots, near, 0)

    for copy in share_x:
        copy.wait_recv()
    row = xbuf[0].astype(f32)
    for i in range(1, xs):
        row = row + xbuf[i].astype(f32)
    wsend[...] = compact(doubled_sum(row))
    zbuf[z] = wsend[...]
    share_z = [
        remote(wsend, zbuf.at[z], z_send, z_recv, o - 1, z_peer(o)) for o in range(1, zs)
    ]

    lax.fori_loop(half_slots, slots // 8, near, 0)

    live = lax.broadcasted_iota(jnp.int32, (leaves, slots), 1) < count[0]
    which = lax.broadcasted_iota(jnp.int32, (leaves, slots), 0) + me * leaves
    pick = ((which == target[...]) & live).astype(f32).astype(bf16)

    def gather_near(step, carry):
        rows = [prod[pl.ds(step * 2 + j, slots, stride=16), :] for j in range(2)]
        high, low = split(jnp.concatenate(rows, axis=1))
        summed = jnp.dot(pick, high, preferred_element_type=f32) + jnp.dot(
            pick, low, preferred_element_type=f32
        )
        for j in range(2):
            start = pl.multiple_of((step * 2 + j) * leaves, leaves)
            nbuf[pl.ds(start, leaves), :] = summed[:, j * 128 : (j + 1) * 128]
        return carry

    lax.fori_loop(0, 8, gather_near, 0)

    for copy in moment_halo:
        copy.wait_recv()
    lax.fori_loop(0, margin // 8, widen(0), 0)
    lax.fori_loop(0, margin // 8, widen(margin + leaves), 0)

    nfar = far.shape[0]

    def far_field(leaf, carry):
        acc = jnp.zeros((64, 128), f32)
        for f in range(0, nfar, 4):
            acc = acc + times_maps(
                [mwin[inside(far[f + j, leaf] - first, 2 * leaves)] for j in range(4)],
                [big_map(far_couple[f + j, leaf]) for j in range(4)],
            )
        farb[leaf] = fold(acc)[:, :64]
        return carry

    lax.fori_loop(0, leaves, far_field, 0)

    for copy in share_z:
        copy.wait_recv()
    for copy in box_z:
        copy.wait_recv()
    row = zbuf[0].astype(f32)
    for i in range(1, zs):
        row = row + zbuf[i].astype(f32)
    high_g, low_g = split(doubled_sum(row))
    down = lax.dot_general(
        jnp.concatenate([high_g, low_g], axis=0), small_t[ntrans + dtrans], NT, preferred_element_type=f32
    )
    listed = [inside(dev_list[0, n] - g * per_group, per_group) for n in range(4)]
    rows = jnp.concatenate([bbuf[b] for b in listed], axis=0)
    beside = fold(
        times_maps(spread(rows, matrix), [big_map(dev_couple[0, n]) for n in range(4)])
    )
    down = down[:16] + down[16:]
    high_b, low_b = split(jnp.concatenate([down, down], axis=1) + beside)
    both = jnp.concatenate([high_b, low_b], axis=0)
    for t in range(ntrans):
        y = lax.dot_general(both, small_t[t], NT, preferred_element_type=f32)
        ybuf[t] = y[:16] + y[16:]

    def finish(step, carry):
        for j in range(4):
            leaf = step * 4 + j
            rounded = (ybuf[leaf_trans[leaf]] + farb[leaf]).astype(bf16)
            out[leaf] = nbuf[pl.ds(leaf, 16, stride=leaves), :] + jnp.dot(
                rounded, bt[leaf], preferred_element_type=f32
            )
        return carry

    lax.fori_loop(0, leaves // 4, finish, 0)

    for copy in to_groups + box_x + charge_halo + moment_halo + share_x + box_z + share_z:
        copy.wait_send()


def local(
    sizes,
    charges,
    leaf_basis,
    near_blocks,
    near_target,
    near_source,
    near_count,
    leaf_far,
    leaf_far_couple,
    leaf_trans,
    dev_trans,
    dev_list,
    dev_couple,
    grp_couple,
    trans_leaf,
    trans_dev,
    couple_table,
):
    groups, zs, xs = sizes
    leaves, r, panels = charges.shape
    slots = near_blocks.shape[0]
    types, k, _ = couple_table.shape
    ntrans = trans_leaf.shape[0]
    width = 2 * leaves
    hbm = pl.BlockSpec(memory_space=pl.ANY)
    smem = pl.BlockSpec(memory_space=pltpu.SMEM)
    vmem = pl.BlockSpec(memory_space=pltpu.VMEM)
    dma = pltpu.SemaphoreType.DMA
    return pl.pallas_call(
        functools.partial(kernel, sizes),
        out_shape=jax.ShapeDtypeStruct((leaves, r, panels), f32),
        in_specs=[hbm, hbm, hbm, vmem] + [smem] * 9 + [hbm, hbm, hbm],
        out_specs=vmem,
        scratch_shapes=[
            pltpu.VMEM((width, r, panels), bf16),
            pltpu.VMEM((leaves, k, panels), bf16),
            pltpu.VMEM((slots, panels, panels), bf16),
            pltpu.VMEM((ntrans, k, k), f32),
            pltpu.VMEM((ntrans, k, k), f32),
            pltpu.VMEM((k, k, types), f32),
            pltpu.VMEM((types, 32, 128), f32),
            pltpu.VMEM((2 * ntrans, 32, 128), f32),
            pltpu.VMEM((2 * ntrans, k, 128), bf16),
            pltpu.VMEM((width, r, 128), bf16),
            pltpu.VMEM((width, 64, 128), bf16),
            pltpu.VMEM((groups, r, 128), bf16),
            pltpu.VMEM((xs, r, 128), bf16),
            pltpu.VMEM((zs, r, 128), bf16),
            pltpu.VMEM((zs * xs, r, 128), bf16),
            pltpu.VMEM((r, 128), bf16),
            pltpu.VMEM((r, 128), bf16),
            pltpu.VMEM((r, 128), bf16),
            pltpu.VMEM((slots * r, panels), f32),
            pltpu.VMEM((r * leaves, panels), f32),
            pltpu.VMEM((leaves, r, k), f32),
            pltpu.VMEM((ntrans, r, k), f32),
            dma((5,)),
            dma((8,)),
            dma((4,)),
            dma((4,)),
            dma((groups - 1,)),
            dma((groups - 1,)),
            dma((xs - 1,)),
            dma((xs - 1,)),
            dma((xs - 1,)),
            dma((xs - 1,)),
            dma((zs - 1,)),
            dma((zs - 1,)),
            dma((zs - 1,)),
            dma((zs - 1,)),
        ],
        compiler_params=pltpu.CompilerParams(collective_id=0, has_side_effects=True),
    )(
        charges,
        jnp.swapaxes(leaf_basis, 1, 2),
        near_blocks,
        near_target.reshape(1, slots),
        near_source,
        near_count,
        leaf_far.T,
        leaf_far_couple.T,
        leaf_trans,
        dev_trans,
        dev_list,
        dev_couple,
        grp_couple,
        trans_leaf,
        trans_dev,
        jnp.transpose(couple_table, (1, 2, 0)),
    )


def solution(mesh):
    groups, per_group = mesh.shape["grp"], mesh.shape["dev"]
    xs = 4 if per_group % 4 == 0 and per_group > 4 else 2
    both = ("grp", "dev")
    return jax.shard_map(
        functools.partial(local, (groups, per_group // xs, xs)),
        mesh=mesh,
        in_specs=(
            P(both, None, None),
            P(both, None, None),
            P(both, None, None),
            P(both),
            P(both),
            P(both),
            P(both, None),
            P(both, None),
            P(both),
            P(both),
            P(both, None),
            P(both, None),
            P(),
            P(),
            P(),
            P(),
        ),
        out_specs=P(both, None, None),
        check_vma=False,
    )
```

time: 210 us -> 41.9 us (0.20)
  blocking collectives: 74.2 us -> 0 us
  local copies, waits for them, and re-layouts: 60.9 us -> 1.67 us
  Pallas kernels: 0 us -> 38.7 us
  matrix products: 32.5 us -> 0 us
  starting transfers between devices: 21.9 us -> 0 us
  between operations: 15 us -> 1.3 us
  other arithmetic: 4.47 us -> 0 us
    unnamed x1 -> x0, blocking collectives: 74.2 us -> none
    gather x8 -> x0, local copies, waits for them, and re-layouts: 44.4 us -> none  [the longest x1 25 us: local(): couple_table[leaf_far_couple]]
    pallas_call x0 -> x1, Pallas kernels: none -> 38.7 us  [local(): pl.pallas_call(functools.partial(kernel, sizes), out_shape=jax.ShapeDtype...]
    dot_general x11 -> x0, matrix products: 32.5 us -> none  [the longest x1 12.1 us: local(): jnp.einsum('lfrk,lfkj->lrj', far_moments, couple_table[leaf_far_couple],...]
    ppermute x4 -> x0, starting transfers between devices: 21.9 us -> none  [the longest x2 16 us: padded(): lax.ppermute(lax.slice_in_dim(block, 0, width, axis=dim), axis, backward)]
    unnamed x27 -> x1, local copies, waits for them, and re-layouts: 12.8 us -> 1.67 us
  transfers between devices with their start and end apart: 5 -> 0, of which waited for: 0 -> 0; matrix products, arithmetic and copies ran while one was open for 32% -> 0% of each run, Pallas kernels for 0% -> 0%
where the time goes in v1:
time: 41.9 us; the launch traced here: 41.7 us
  Pallas kernels  38.7 us (92%)
  local copies, waits for them, and re-layouts  1.67 us (4%)
  between operations  1.3 us (3%)
    pallas_call x1, Pallas kernels, local(): pl.pallas_call(functools.partial(kernel, sizes), out_shape=jax.ShapeDtype...  38.7 us
    unnamed x1, local copies, waits for them, and re-layouts  1.67 us

profile of v1, /device:TPU:1, one launch (start us, length us, event | category | flops | bytes accessed | tf_op | source)
XLA Modules:
  0.0 41.7 jit_solution(14146282107472706432)
XLA Ops:
  1.3 38.7 %shard_map.154 = f32[32,16,128]{2,1,0:T(8,128)} custom-call(bf16[32,16,128]{2,1,0:T(8,128)(2,1)} %charges.1, bf16[32,64,128]{2,1,0:T(8,128)(2,1)} %bitcast.6, bf16[160,128,128]{2,1,0:T(8,128)(2,1)} %blocks.1, s32[1,160]{1,0:T(1,128)} %bitcast.9, s32[160]{0:T(256)} %source.1, s32[1]{0:T(128)S(6)} %copy.18.count, s32[16,32]{1,0:T(8,128)} %bitcast.7, ...), custom_call_target="tpu_custom_call" | custom-call | tf_op jit(solution)/shard_map/pallas_call | solution.py:441
  40.0 1.7 %copy.20 = f32[32,16,128]{2,1,0:T(8,128)} copy(f32[32,16,128]{2,1,0:T(8,128)} %shard_map.154) | data formatting | bytes 524288

commit v2 on v1

--- a/solution.py
+++ b/solution.py
@@ -9,6 +9,17 @@
 
 f32, bf16 = jnp.float32, jnp.bfloat16
 MESH = pl.DeviceIdType.MESH
+TABLE_PITCH = 40
+PROD_PITCH = 24
+NEAR_PITCH = 40
+U_MOM = 16
+U_WIDE = 16
+U_BOX = 16
+U_TURN = 2
+U_NEAR = 16
+U_GATHER = 2
+U_FAR = 4
+U_FIN = 8
 NT = (((1,), (1,)), ((), ()))
 
 
@@ -134,7 +145,7 @@
     margin = leaves // 2
     slots = blk.shape[0]
     types = table.shape[0]
-    rows_of = table.reshape(types * 32, 128)
+    rows_of = table.reshape(types * TABLE_PITCH, 128)
     ntrans = tl.shape[0]
     chunks = 4
     per_chunk = 32 // chunks
@@ -200,8 +211,8 @@
     loads[1].wait()
 
     def moments(step, carry):
-        for j in range(8):
-            leaf = step * 8 + j
+        for j in range(U_MOM):
+            leaf = step * U_MOM + j
             b = bt[leaf]
             m = lax.dot_general(
                 window[margin + leaf],
@@ -212,32 +223,34 @@
             cwin[margin + leaf] = compact(m)
         return carry
 
-    lax.fori_loop(0, leaves // 8, moments, 0)
+    lax.fori_loop(0, leaves // U_MOM, moments, 0)
 
     def widen(start):
         def body(step, carry):
-            c = jnp.concatenate([cwin[start + step * 8 + j] for j in range(8)], axis=0)
+            c = jnp.concatenate([cwin[start + step * U_WIDE + j] for j in range(U_WIDE)], axis=0)
             for j, w in enumerate(spread(c, matrix)):
-                mwin[start + step * 8 + j] = w
+                mwin[start + step * U_WIDE + j] = w
             return carry
 
         return body
 
-    lax.fori_loop(0, leaves // 8, widen(margin), 0)
+    lax.fori_loop(0, leaves // U_WIDE, widen(margin), 0)
 
     def small_map(i):
         return small[i]
 
     def big_map(i):
-        return table[i]
+        return table[i][:32]
 
     def to_box(step, carry):
-        picks = [step * 4 + j for j in range(4)]
-        return carry + times_maps(
-            [mwin[margin + p] for p in picks], [small_map(leaf_trans[p]) for p in picks]
-        )
-
-    box = compact(fold(lax.fori_loop(0, leaves // 4, to_box, jnp.zeros((64, 128), f32))))
+        for i in range(0, U_BOX, 4):
+            picks = [step * U_BOX + i + j for j in range(4)]
+            carry = carry + times_maps(
+                [mwin[margin + p] for p in picks], [small_map(leaf_trans[p]) for p in picks]
+            )
+        return carry
+
+    box = compact(fold(lax.fori_loop(0, leaves // U_BOX, to_box, jnp.zeros((64, 128), f32))))
     bbuf[d] = box
     dtrans = dev_trans[0]
     usend[...] = compact(fold(times_maps(spread(box, matrix), [small_map(ntrans + dtrans)])))
@@ -280,12 +293,13 @@
         raw_loads[2 * c + 1].wait()
 
         def turn(i, carry):
-            k = c * per_chunk + i
-            both = jnp.concatenate([raw[k], raw[k + 32]], axis=0)
-            rows_of[pl.ds(k, types, stride=32), :] = both.T
+            for j in range(U_TURN):
+                k = c * per_chunk + i * U_TURN + j
+                both = jnp.concatenate([raw[k], raw[k + 32]], axis=0)
+                rows_of[pl.ds(k, types, stride=TABLE_PITCH), :] = both.T
             return carry
 
-        lax.fori_loop(0, per_chunk, turn, 0)
+        lax.fori_loop(0, per_chunk // U_TURN, turn, 0)
 
     for copy in to_groups:
         copy.wait_recv()
@@ -311,15 +325,15 @@
     block_load.wait()
 
     def near(step, carry):
-        for j in range(8):
-            s = step * 8 + j
+        for j in range(U_NEAR):
+            s = step * U_NEAR + j
             product = lax.dot_general(
                 window[inside(source[s] - first, 2 * leaves)], blk[s], NT, preferred_element_type=f32
             )
-            prod[pl.ds(pl.multiple_of(s * 16, 16), 16), :] = product
+            prod[pl.ds(pl.multiple_of(s * PROD_PITCH, 8), 16), :] = product
         return carry
 
-    half_slots = slots // 16
+    half_slots = slots // U_NEAR // 2
     lax.fori_loop(0, half_slots, near, 0)
 
     for copy in share_x:
@@ -333,43 +347,47 @@
         remote(wsend, zbuf.at[z], z_send, z_recv, o - 1, z_peer(o)) for o in range(1, zs)
     ]
 
-    lax.fori_loop(half_slots, slots // 8, near, 0)
+    lax.fori_loop(half_slots, slots // U_NEAR, near, 0)
 
     live = lax.broadcasted_iota(jnp.int32, (leaves, slots), 1) < count[0]
     which = lax.broadcasted_iota(jnp.int32, (leaves, slots), 0) + me * leaves
     pick = ((which == target[...]) & live).astype(f32).astype(bf16)
 
     def gather_near(step, carry):
-        rows = [prod[pl.ds(step * 2 + j, slots, stride=16), :] for j in range(2)]
-        high, low = split(jnp.concatenate(rows, axis=1))
-        summed = jnp.dot(pick, high, preferred_element_type=f32) + jnp.dot(
-            pick, low, preferred_element_type=f32
-        )
-        for j in range(2):
-            start = pl.multiple_of((step * 2 + j) * leaves, leaves)
-            nbuf[pl.ds(start, leaves), :] = summed[:, j * 128 : (j + 1) * 128]
+        for i in range(U_GATHER):
+            first_row = (step * U_GATHER + i) * 2
+            rows = [prod[pl.ds(first_row + j, slots, stride=PROD_PITCH), :] for j in range(2)]
+            high, low = split(jnp.concatenate(rows, axis=1))
+            summed = jnp.dot(pick, high, preferred_element_type=f32) + jnp.dot(
+                pick, low, preferred_element_type=f32
+            )
+            for j in range(2):
+                start = pl.multiple_of((first_row + j) * NEAR_PITCH, 8)
+                nbuf[pl.ds(start, leaves), :] = summed[:, j * 128 : (j + 1) * 128]
         return carry
 
-    lax.fori_loop(0, 8, gather_near, 0)
+    lax.fori_loop(0, 8 // U_GATHER, gather_near, 0)
 
     for copy in moment_halo:
         copy.wait_recv()
-    lax.fori_loop(0, margin // 8, widen(0), 0)
-    lax.fori_loop(0, margin // 8, widen(margin + leaves), 0)
+    lax.fori_loop(0, margin // U_WIDE, widen(0), 0)
+    lax.fori_loop(0, margin // U_WIDE, widen(margin + leaves), 0)
 
     nfar = far.shape[0]
 
-    def far_field(leaf, carry):
-        acc = jnp.zeros((64, 128), f32)
-        for f in range(0, nfar, 4):
-            acc = acc + times_maps(
-                [mwin[inside(far[f + j, leaf] - first, 2 * leaves)] for j in range(4)],
-                [big_map(far_couple[f + j, leaf]) for j in range(4)],
-            )
-        farb[leaf] = fold(acc)[:, :64]
+    def far_field(step, carry):
+        for i in range(U_FAR):
+            leaf = step * U_FAR + i
+            acc = jnp.zeros((64, 128), f32)
+            for f in range(0, nfar, 4):
+                acc = acc + times_maps(
+                    [mwin[inside(far[f + j, leaf] - first, 2 * leaves)] for j in range(4)],
+                    [big_map(far_couple[f + j, leaf]) for j in range(4)],
+                )
+            farb[leaf] = fold(acc)[:, :64]
         return carry
 
-    lax.fori_loop(0, leaves, far_field, 0)
+    lax.fori_loop(0, leaves // U_FAR, far_field, 0)
 
     for copy in share_z:
         copy.wait_recv()
@@ -395,15 +413,15 @@
         ybuf[t] = y[:16] + y[16:]
 
     def finish(step, carry):
-        for j in range(4):
-            leaf = step * 4 + j
+        for j in range(U_FIN):
+            leaf = step * U_FIN + j
             rounded = (ybuf[leaf_trans[leaf]] + farb[leaf]).astype(bf16)
-            out[leaf] = nbuf[pl.ds(leaf, 16, stride=leaves), :] + jnp.dot(
+            out[leaf] = nbuf[pl.ds(leaf, 16, stride=NEAR_PITCH), :] + jnp.dot(
                 rounded, bt[leaf], preferred_element_type=f32
             )
         return carry
 
-    lax.fori_loop(0, leaves // 4, finish, 0)
+    lax.fori_loop(0, leaves // U_FIN, finish, 0)
 
     for copy in to_groups + box_x + charge_halo + moment_halo + share_x + box_z + share_z:
         copy.wait_send()
@@ -450,7 +468,7 @@
             pltpu.VMEM((ntrans, k, k), f32),
             pltpu.VMEM((ntrans, k, k), f32),
             pltpu.VMEM((k, k, types), f32),
-            pltpu.VMEM((types, 32, 128), f32),
+            pltpu.VMEM((types, TABLE_PITCH, 128), f32),
             pltpu.VMEM((2 * ntrans, 32, 128), f32),
             pltpu.VMEM((2 * ntrans, k, 128), bf16),
             pltpu.VMEM((width, r, 128), bf16),
@@ -462,8 +480,8 @@
             pltpu.VMEM((r, 128), bf16),
             pltpu.VMEM((r, 128), bf16),
             pltpu.VMEM((r, 128), bf16),
-            pltpu.VMEM((slots * r, panels), f32),
-            pltpu.VMEM((r * leaves, panels), f32),
+            pltpu.VMEM((slots * PROD_PITCH, panels), f32),
+            pltpu.VMEM((r * NEAR_PITCH, panels), f32),
             pltpu.VMEM((leaves, r, k), f32),
             pltpu.VMEM((ntrans, r, k), f32),
             dma((5,)),

time: 41.9 us -> 33.5 us (0.80)
  Pallas kernels: 38.7 us -> 30.4 us
    pallas_call x1, Pallas kernels: 38.7 us -> 30.4 us  [local(): pl.pallas_call(functools.partial(kernel, sizes), out_shape=jax.ShapeDtype...]
where the time goes in v2:
time: 33.5 us; the launch traced here: 33.4 us
  Pallas kernels  30.4 us (91%)
  local copies, waits for them, and re-layouts  1.67 us (5%)
  between operations  1.3 us (4%)
    pallas_call x1, Pallas kernels, local(): pl.pallas_call(functools.partial(kernel, sizes), out_shape=jax.ShapeDtype...  30.4 us
    unnamed x1, local copies, waits for them, and re-layouts  1.67 us

profile of v2, /device:TPU:1, one launch (start us, length us, event | category | flops | bytes accessed | tf_op | source)
XLA Modules:
  0.0 33.4 jit_solution(8363424019232334828)
XLA Ops:
  1.3 30.4 %shard_map.154 = f32[32,16,128]{2,1,0:T(8,128)} custom-call(bf16[32,16,128]{2,1,0:T(8,128)(2,1)} %charges.1, bf16[32,64,128]{2,1,0:T(8,128)(2,1)} %bitcast.6, bf16[160,128,128]{2,1,0:T(8,128)(2,1)} %blocks.1, s32[1,160]{1,0:T(1,128)} %bitcast.9, s32[160]{0:T(256)} %source.1, s32[1]{0:T(128)S(6)} %copy.18.count, s32[16,32]{1,0:T(8,128)} %bitcast.7, ...), custom_call_target="tpu_custom_call" | custom-call | tf_op jit(solution)/shard_map/pallas_call | solution.py:459
  31.7 1.7 %copy.20 = f32[32,16,128]{2,1,0:T(8,128)} copy(f32[32,16,128]{2,1,0:T(8,128)} %shard_map.154) | data formatting | bytes 524288
